TPU v7x, 32 devices: a whole 2x2x4 slice. The times are simulated.
32 devices in a mesh: frame: 8 (over y, x, core), tensor: 4 (over z).
Axes of the slice: x: 2, y: 2, z: 4, core: 2. Of those that a mesh axis runs over, the one named last changes fastest.
Arguments:
- tokens: bfloat16 [1024, 1, 4096], P(('frame', 'tensor')), may hold values from -6 to 6
- norm_gain: float32 [4096], replicated, may hold values from 0.5 to 1.5
- query_weight: bfloat16 [4096, 4096], P(None, 'tensor'), may hold values from -0.09375 to 0.09375
- out_weight: bfloat16 [4096, 4096], P('tensor'), may hold values from -0.09375 to 0.09375
- cache_keys: bfloat16 [384, 1, 4096], P('frame', None, 'tensor'), may hold values from -420 to 420
- cache_values: bfloat16 [384, 1, 4096], P('frame', None, 'tensor'), may hold values from -18 to 18
- token_pos: int32 [1024, 1], P('frame'), may hold values from 0 to 383, as said below
- frame_pad: int32 [1], replicated, may hold values from 0 to 192
Outputs:
- mixed: bfloat16 [1024, 1, 4096], P(('frame', 'tensor'))
Inputs may be any that keep to these rules, and one draw needn't show every extreme that they name: `token_pos`: nondecreasing along each sequence; the last token of every sequence has 383.
All inputs are finite; a program needn't handle non-finite values.
Results may differ from a plain program's by a relative error of at most 0.018.
Values may be sent and summed in bfloat16 or wider, within the bound.
A program may use at most 64 MiB of HBM per device.

v0:
```python
import jax
import jax.numpy as jnp
from jax import lax
from jax.sharding import PartitionSpec as P

HEAD_DIM = 128
epsilon = 1e-06
masked_score = -1e30


def normalize(block_rows, norm_gain):
    hidden = block_rows.astype(jnp.float32)
    factor = lax.rsqrt(jnp.mean(hidden * hidden, axis=-1, keepdims=True) + epsilon)
    return (hidden * factor * norm_gain).astype(jnp.bfloat16)


def per_device(
    tokens, norm_gain, query_weight, out_weight, cache_keys, cache_values, token_pos, frame_pad
):
    head_cols = query_weight.shape[1]
    heads_here = head_cols // HEAD_DIM
    seq_count = tokens.shape[1]
    query_scale = HEAD_DIM ** (-0.5)
    normed = normalize(lax.all_gather(tokens, "tensor", axis=0, tiled=True), norm_gain)
    queries = (
        jnp.dot(normed, query_weight, preferred_element_type=jnp.float32) * query_scale
    ).astype(jnp.bfloat16)
    query_rows = queries.shape[0]
    query_heads = queries.reshape(query_rows, seq_count, heads_here, HEAD_DIM)
    all_frames = cache_keys.shape[0] * lax.axis_size("frame")
    valid_frames = all_frames - frame_pad
    start_max = jnp.full((query_rows, seq_count, heads_here), masked_score, jnp.float32)
    running_max = start_max
    key_piece = lax.all_gather(cache_keys, "frame", axis=0, tiled=True)
    value_piece = lax.all_gather(cache_values, "frame", axis=0, tiled=True)
    row_count = key_piece.shape[0]
    frame_index = jnp.arange(row_count, dtype=jnp.int32)
    visible = (frame_index[None, None, :] <= token_pos[:, :, None]) & (
        frame_index[None, None, :] < valid_frames[None, :, None]
    )
    key_heads = key_piece.reshape(row_count, seq_count, heads_here, HEAD_DIM)
    scores = jnp.einsum(
        "rshd,fshd->rshf", query_heads, key_heads, preferred_element_type=jnp.float32
    )
    visible = visible[:, :, None, :]
    scores, visible = (jnp.where(visible, scores, masked_score), visible)
    new_max = jnp.maximum(running_max, jnp.max(scores, axis=-1))
    weights = jnp.where(visible, jnp.exp(scores - new_max[..., None]), 0.0)
    running_sum = jnp.sum(weights, axis=-1)
    value_heads = value_piece.reshape(value_piece.shape[0], seq_count, heads_here, HEAD_DIM)
    accumulated = jnp.einsum(
        "rshf,fshd->rshd",
        weights.astype(jnp.bfloat16),
        value_heads,
        preferred_element_type=jnp.float32,
    )
    running_max, running_sum, accumulated = (new_max, running_sum, accumulated)
    attended = (
        (accumulated / running_sum[..., None])
        .astype(jnp.bfloat16)
        .reshape(query_rows, seq_count, head_cols)
    )
    return lax.psum_scatter(
        jnp.dot(attended, out_weight, preferred_element_type=jnp.float32).astype(jnp.bfloat16),
        "tensor",
        scatter_dimension=0,
        tiled=True,
    )


def solution(mesh):
    placed = (
        P(("frame", "tensor"), None, None),
        P(),
        P(None, "tensor"),
        P("tensor", None),
        P("frame", None, "tensor"),
        P("frame", None, "tensor"),
        P("frame", None),
        P(),
    )
    return jax.shard_map(
        per_device,
        mesh=mesh,
        in_specs=placed,
        out_specs=P(("frame", "tensor"), None, None),
        check_vma=False,
    )
```

profile of v0, /device:TPU:0, one launch (start us, length us, event | category | flops | bytes accessed | tf_op | source)
XLA Modules:
  0.0 84.1 jit_solution(8908072664769119444)
XLA Ops:
  6.5 0.0 copy-start
  6.5 0.0 all-gather.2.cloned.1.call-start
  6.5 0.7 all-gather.2.cloned.1.call-update
  7.3 0.0 reduce-scatter.2.cloned.1.call-start
  8.0 12.2 %all_gather.10 = bf16[384,1,1024]{2,0,1:T(8,128)(2,1)S(1)} all-gather(bf16[48,1,1024]{2,0,1:T(8,128)(2,1)} %param.12), channel_id=1, replica_groups=mesh['frame'=8,'tensor'=4] {'frame'}, dimensions={0}, use_global_device_ids=true | all-gather | bytes 884736 | tf_op jit(solution)/shard_map/all_gather | solution.py:34
  20.2 0.4 copy.15
  20.5 0.0 copy-done
  20.6 0.0 copy-start.1
  20.6 0.0 copy-start.2
  20.6 10.0 %all_gather.11 = bf16[384,1,1024]{2,0,1:T(8,128)(2,1)S(1)} all-gather(bf16[48,1,1024]{2,0,1:T(8,128)(2,1)S(1)} %copy-done), channel_id=1, replica_groups=mesh['frame'=8,'tensor'=4] {'frame'}, dimensions={0}, use_global_device_ids=true | all-gather | bytes 884736 | tf_op jit(solution)/shard_map/all_gather | solution.py:35
  30.6 0.4 copy.18
  31.0 0.0 copy-done.1
  31.0 0.1 fusion.21
  31.1 8.5 %all-gather.2.cloned.1.call-done = bf16[128,1,4096]{2,0,1:T(8,128)(2,1)} async-done(((bf16[32,1,4096]{2,0,1:T(8,128)(2,1)}), bf16[128,1,4096]{2,0,1:T(8,128)(2,1)}) %all-gather.2.cloned.1.call-update) | async-done | bytes 1048592 | tf_op jit(solution)/shard_map/all_gather | solution.py:24
  39.6 0.0 slice-start
  39.6 1.7 %fusion.1 = f32[128]{0:T(128)S(1)} fusion(bf16[128,1,4096]{2,0,1:T(8,128)(2,1)} %all-gather.2.cloned.1.call-done), kind=kLoop, calls=%fused_computation.4 | loop fusion | flops 1572736 | bytes 1049088 | tf_op jit(solution)/shard_map/reduce_sum | solution.py:13
  41.3 0.0 copy-done.2
  41.3 0.0 slice-start.1
  41.3 5.2 %fusion.7 = bf16[16,8,8,128]{3,2,1,0:T(8,128)(2,1)S(1)} fusion(bf16[4096,1024]{1,0:T(8,128)(2,1)} %param.10, bf16[128,1,4096]{2,0,1:T(8,128)(2,1)} %all-gather.2.cloned.1.call-done, f32[4096]{0:T(1024)S(1)} %copy-done.2, f32[128]{0:T(128)S(1)} %add_rsqrt_fusion), kind=kOutput, calls=%fused_computation.14 | convolution fusion | flops 1076101120 | bytes 9716224 | tf_op jit(solution)/shard_map/dot_general | solution.py:26
  46.5 0.5 fusion.23
  47.0 0.6 fusion.4
  47.6 0.6 fusion.13
  48.1 0.0 slice-done
  48.2 0.0 slice-done.1
  48.2 2.3 %fusion = bf16[128,1,4096]{2,0,1:T(8,128)(2,1)} fusion(bf16[128,1024]{0,1:T(8,128)(2,1)S(1)} %bitcast.45, bf16[1024,4096]{1,0:T(8,128)(2,1)S(1)} %bitcast.42), kind=kOutput, calls=%fused_computation.1 | convolution fusion | flops 1074266112 | bytes 9699328 | tf_op jit(solution)/shard_map/dot_general | solution.py:64
  50.4 0.0 reduce-scatter.2.cloned.1.call-update
  50.5 26.8 %reduce-scatter.2.cloned.1.call-done = bf16[32,1,4096]{2,0,1:T(8,128)(2,1)} async-done(((bf16[128,1,4096]{2,0,1:T(8,128)(2,1)}), bf16[32,1,4096]{2,0,1:T(8,128)(2,1)}) %reduce-scatter.2.cloned.1.call-update) | async-done | bytes 262160 | tf_op jit(solution)/shard_map/reduce_scatter | solution.py:63
  (4 shorter events, 0.0 us)
Async XLA Ops:
  6.5 14.0 %copy-start = (bf16[48,1,1024]{2,0,1:T(8,128)(2,1)S(1)}, bf16[48,1,1024]{2,0,1:T(8,128)(2,1)}, u32[]{:S(2)}) copy-start(bf16[48,1,1024]{2,0,1:T(8,128)(2,1)} %param.13) | copy-start | bytes 294916
  6.5 33.1 %all-gather.2.cloned.1.call-start = ((), (), s32[]{:S(2)}) async-start(), calls=%async_computation.1 | async-start | bytes 1310720 | tf_op jit(solution)/shard_map/all_gather | solution.py:24
  7.3 70.0 %reduce-scatter.2.cloned.1.call-start = ((), (), s32[]{:S(2)}) async-start(), calls=%async_computation.2 | async-start | bytes 1310720 | tf_op jit(solution)/shard_map/reduce_scatter | solution.py:63
  20.6 10.4 %copy-start.1 = (s32[128,1]{0,1:T(1,128)S(1)}, s32[128,1]{0,1:T(1,128)}, u32[]{:S(2)}) copy-start(s32[128,1]{0,1:T(1,128)} %param.14) | copy-start | bytes 1540
  20.6 20.8 %copy-start.2 = (f32[4096]{0:T(1024)S(1)}, f32[4096]{0:T(1024)}, u32[]{:S(2)}) copy-start(f32[4096]{0:T(1024)} %param.9) | copy-start | bytes 49156
  39.6 8.5 %slice-start = ((s8[8388608]{0:T(1024)(128)(4,1)}), s8[4194304]{0:T(1024)(128)(4,1)S(1)}, s32[]{:S(2)}) async-start(s8[8388608]{0:T(1024)(128)(4,1)} %bitcast.41), calls=%async_computation.3 | async-start | bytes 8388608
  41.3 6.8 %slice-start.1 = ((s8[8388608]{0:T(1024)(128)(4,1)}), s8[4194304]{0:T(1024)(128)(4,1)S(1)}, s32[]{:S(2)}) async-start(s8[8388608]{0:T(1024)(128)(4,1)} %bitcast.41), calls=%async_computation.4 | async-start | bytes 8388608
Sparse Core Ops, SparseCore 0:
  8.9 30.6 all-gather.1
  50.6 26.6 reduce-scatter.1
where the time goes:
time: 84.3 us; the launch traced here: 84.1 us
  waiting for transfers between devices  36.1 us (43%)
  blocking collectives  22.3 us (26%)
  between operations  14.2 us (17%)
  matrix products  8.47 us (10%)
  other arithmetic  2.36 us (3%)
    reduce_scatter x1, waiting for transfers between devices, per_device(): lax.psum_scatter(jnp.dot(attended, out_weight, preferred_element_type=jnp...  26.8 us
    all_gather x1, blocking collectives, per_device(): key_piece = lax.all_gather(cache_keys, 'frame', axis=0, tiled=True)  12.2 us
    all_gather x1, blocking collectives, per_device(): value_piece = lax.all_gather(cache_values, 'frame', axis=0, tiled=True)  10 us
    all_gather x1, waiting for transfers between devices, per_device(): lax.all_gather(tokens, 'tensor', axis=0, tiled=True)  8.55 us
    dot_general x1, matrix products, per_device(): jnp.dot(normed, query_weight, preferred_element_type=jnp.float32)  5.17 us
    dot_general x1, matrix products, per_device(): jnp.dot(attended, out_weight, preferred_element_type=jnp.float32)  2.26 us
  transfers between devices with their start and end apart: 2, of which 2 were waited for; matrix products, arithmetic and copies ran while one was open for 1% of the time, Pallas kernels for 0%

commit v1 on v0

--- a/solution.py
+++ b/solution.py
@@ -31,8 +31,13 @@
     valid_frames = all_frames - frame_pad
     start_max = jnp.full((query_rows, seq_count, heads_here), masked_score, jnp.float32)
     running_max = start_max
-    key_piece = lax.all_gather(cache_keys, "frame", axis=0, tiled=True)
-    value_piece = lax.all_gather(cache_values, "frame", axis=0, tiled=True)
+    key_piece, value_piece = jnp.split(
+        lax.all_gather(
+            jnp.concatenate([cache_keys, cache_values], axis=1), "frame", axis=0, tiled=True
+        ),
+        [cache_keys.shape[1]],
+        axis=1,
+    )
     row_count = key_piece.shape[0]
     frame_index = jnp.arange(row_count, dtype=jnp.int32)
     visible = (frame_index[None, None, :] <= token_pos[:, :, None]) & (

time: 84.3 us -> 117 us (1.39)
  waiting for transfers between devices: 36.1 us -> 77.4 us
  blocking collectives: 22.3 us -> 0 us
  local copies, waits for them, and re-layouts: 0.73 us -> 9.78 us
  matrix products: 8.47 us -> 11.5 us
  other arithmetic: 2.36 us -> 3.55 us
    all_gather x2 -> x0, blocking collectives: 22.3 us -> none  [the longest x1 12.2 us: per_device(): key_piece = lax.all_gather(cache_keys, 'frame', axis=0, tiled=True)]
    all_gather x1, waiting for transfers between devices: 8.55 us -> 29 us  [per_device(): lax.all_gather(tokens, 'tensor', axis=0, tiled=True)]
    all_gather x0 -> x1, waiting for transfers between devices: none -> 20.3 us  [per_device(): lax.all_gather(jnp.concatenate([cache_keys, cache_values], axis=1), 'fram...]
    split x0 -> x2, local copies, waits for them, and re-layouts: none -> 7.22 us  [per_device(): jnp.split(lax.all_gather(jnp.concatenate([cache_keys, cache_values], axis...]
    dot_general x1, matrix products: 2.26 us -> 5.66 us  [per_device(): jnp.dot(attended, out_weight, preferred_element_type=jnp.float32)]
    unnamed x10 -> x5, local copies, waits for them, and re-layouts: 0.03 us -> 1.68 us
  transfers between devices with their start and end apart: 2 -> 3, of which waited for: 2 -> 3; matrix products, arithmetic and copies ran while one was open for 1% -> 8% of each run, Pallas kernels for 0% -> 0%
where the time goes in v1:
time: 117 us; the launch traced here: 116 us
  waiting for transfers between devices  77.4 us (66%)
  between operations  13.8 us (12%)
  matrix products  11.5 us (10%)
  local copies, waits for them, and re-layouts  9.78 us (8%)
  other arithmetic  3.55 us (3%)
    all_gather x1, waiting for transfers between devices, per_device(): lax.all_gather(tokens, 'tensor', axis=0, tiled=True)  29 us
    reduce_scatter x1, waiting for transfers between devices, per_device(): lax.psum_scatter(jnp.dot(attended, out_weight, preferred_element_type=jnp...  27.4 us
    all_gather x1, waiting for transfers between devices, per_device(): lax.all_gather(jnp.concatenate([cache_keys, cache_values], axis=1), 'fram...  20.3 us
    split x2, local copies, waits for them, and re-layouts, per_device(): jnp.split(lax.all_gather(jnp.concatenate([cache_keys, cache_values], axis...  7.22 us
    dot_general x1, matrix products, per_device(): jnp.dot(attended, out_weight, preferred_element_type=jnp.float32)  5.66 us
    dot_general x1, matrix products, per_device(): jnp.dot(normed, query_weight, preferred_element_type=jnp.float32)  5.04 us
  transfers between devices with their start and end apart: 3, of which 3 were waited for; matrix products, arithmetic and copies ran while one was open for 8% of the time, Pallas kernels for 0%

profile of v1, /device:TPU:0, one launch (start us, length us, event | category | flops | bytes accessed | tf_op | source)
XLA Modules:
  0.0 116.2 jit_solution(6860940489041761363)
XLA Ops:
  6.5 0.0 copy-start.1
  6.5 0.0 all-gather.5.cloned.1.call-start
  6.5 0.7 all-gather.5.cloned.1.call-update
  7.3 0.0 all-gather.3.cloned.1.call-start
  7.3 1.0 pad_maximum_fusion
  8.3 0.9 copy.17
  9.1 0.0 all-gather.3.cloned.1.call-update
  9.2 0.0 reduce-scatter.2.cloned.1.call-start
  9.9 0.8 fusion.21
  10.7 29.0 %all-gather.5.cloned.1.call-done = bf16[128,1,4096]{2,0,1:T(8,128)(2,1)} async-done(((bf16[32,1,4096]{2,0,1:T(8,128)(2,1)}), bf16[128,1,4096]{2,0,1:T(8,128)(2,1)}) %all-gather.5.cloned.1.call-update) | async-done | bytes 1048592 | tf_op jit(solution)/shard_map/all_gather | solution.py:24
  39.6 1.5 %fusion.1 = f32[128]{0:T(128)S(1)} fusion(bf16[128,1,4096]{2,0,1:T(8,128)(2,1)} %all-gather.5.cloned.1.call-done), kind=kLoop, calls=%fused_computation.4 | loop fusion | flops 1572736 | bytes 1049088 | tf_op jit(solution)/shard_map/reduce_sum | solution.py:13
  41.2 0.0 copy-done.1
  41.2 5.0 %fusion.7 = bf16[16,8,8,128]{3,2,1,0:T(8,128)(2,1)S(1)} fusion(bf16[4096,1024]{1,0:T(8,128)(2,1)} %param.10, bf16[128,1,4096]{2,0,1:T(8,128)(2,1)} %all-gather.5.cloned.1.call-done, f32[4096]{0:T(1024)S(1)} %copy-done.1, f32[128]{0:T(128)S(1)} %add_rsqrt_fusion), kind=kOutput, calls=%fused_computation.14 | convolution fusion | flops 1076101120 | bytes 9716224 | tf_op jit(solution)/shard_map/dot_general | solution.py:26
  46.2 20.3 %all-gather.3.cloned.1.call-done = bf16[384,2,1024]{2,1,0:T(2,128)(2,1)} async-done(((bf16[48,2,1024]{2,1,0:T(2,128)(2,1)}), bf16[384,2,1024]{2,1,0:T(2,128)(2,1)}) %all-gather.3.cloned.1.call-update) | async-done | bytes 1572880 | tf_op jit(solution)/shard_map/all_gather | solution.py:35
  66.5 4.4 %fusion.23 = (bf16[384,1,1024]{2,1,0:T(2,128)(2,1)S(1)}, bf16[384,1,1024]{2,1,0:T(2,128)(2,1)S(1)}) fusion(bf16[384,2,1024]{2,1,0:T(2,128)(2,1)} %all-gather.3.cloned.1.call-done), kind=kLoop, calls=%fused_computation.33 | loop fusion | bytes 3145728 | tf_op jit(solution)/shard_map/split | solution.py:34
  70.9 2.8 %copy.18 = bf16[384,1,1024]{0,2,1:T(8,128)(2,1)} copy(bf16[384,1,1024]{2,1,0:T(2,128)(2,1)S(1)} %get-tuple-element.6) | data formatting | bytes 1572864 | tf_op jit(solution)/shard_map/split | solution.py:34
  73.7 1.3 %copy.25 = bf16[384,1,1024]{0,2,1:T(8,128)(2,1)S(1)} copy(bf16[384,1,1024]{2,1,0:T(2,128)(2,1)S(1)} %get-tuple-element.5) | data formatting | bytes 1572864
  75.0 0.0 copy-start
  75.0 0.4 fusion.24
  75.5 0.3 fusion.4
  75.8 0.4 copy-done
  76.2 0.4 fusion.13
  76.6 5.7 %fusion = bf16[128,1,4096]{2,0,1:T(8,128)(2,1)} fusion(bf16[128,1024]{0,1:T(8,128)(2,1)S(1)} %bitcast.39, bf16[1024,4096]{1,0:T(8,128)(2,1)} %param.11), kind=kOutput, calls=%fused_computation.1 | convolution fusion | flops 1074266112 | bytes 9699328 | tf_op jit(solution)/shard_map/dot_general | solution.py:69
  82.2 0.0 reduce-scatter.2.cloned.1.call-update
  82.3 27.4 %reduce-scatter.2.cloned.1.call-done = bf16[32,1,4096]{2,0,1:T(8,128)(2,1)} async-done(((bf16[128,1,4096]{2,0,1:T(8,128)(2,1)}), bf16[32,1,4096]{2,0,1:T(8,128)(2,1)}) %reduce-scatter.2.cloned.1.call-update) | async-done | bytes 262160 | tf_op jit(solution)/shard_map/reduce_scatter | solution.py:68
  (3 shorter events, 0.0 us)
Async XLA Ops:
  6.5 34.6 %copy-start.1 = (f32[4096]{0:T(1024)S(1)}, f32[4096]{0:T(1024)}, u32[]{:S(2)}) copy-start(f32[4096]{0:T(1024)} %param.9) | copy-start | bytes 49156
  6.5 33.1 %all-gather.5.cloned.1.call-start = ((), (), s32[]{:S(2)}) async-start(), calls=%async_computation.2 | async-start | bytes 1310720 | tf_op jit(solution)/shard_map/all_gather | solution.py:24
  7.3 59.2 %all-gather.3.cloned.1.call-start = ((), (), s32[]{:S(2)}) async-start(), calls=%async_computation.1 | async-start | bytes 1769472 | tf_op jit(solution)/shard_map/all_gather | solution.py:35
  9.2 100.5 %reduce-scatter.2.cloned.1.call-start = ((), (), s32[]{:S(2)}) async-start(), calls=%async_computation.3 | async-start | bytes 1310720 | tf_op jit(solution)/shard_map/reduce_scatter | solution.py:68
  75.0 1.1 copy-start
Sparse Core Ops, SparseCore 0:
  8.9 30.6 all-gather.4
  41.5 24.9 all-gather.2
  82.4 27.2 reduce-scatter.1
